TPU v7x, 32 devices: a whole 2x2x4 slice. The times are simulated.
32 devices in a mesh: groups: 1, ex: 16 (over z, y, core), layer: 2 (over x), pb: 1.
Axes of the slice: x: 2, y: 2, z: 4, core: 2. Of those that a mesh axis runs over, the one named last changes fastest.
Arguments:
- train_grads: float32 [2, 1536, 1024], P('layer', ('groups', 'ex')), may hold values from -64 to 64
- query_grads: float32 [2, 1, 512, 1024], P('layer', 'pb', ('groups', 'ex')), may hold values from -64 to 64
- damping: float32 [2], P('layer'), may hold values from 0.05 to 0.5
Outputs:
- influence: float32 [1536, 1, 512], P(('groups', 'ex'), 'pb', 'layer')
All inputs are finite; a program needn't handle non-finite values.
Results may differ from a plain program's by a relative error of at most 0.0003.
Values sent between devices are 32-bit elements; how exact they have to be, the bound alone decides.
A program may use at most 64 MiB of HBM per device.

v0:
```python
import jax
import jax.numpy as jnp
from jax import lax
from jax.sharding import PartitionSpec as P


def solve_rows(factor, rows_in):
    inner = lax.linalg.triangular_solve(
        factor, rows_in, left_side=False, lower=True, transpose_a=True
    )
    return lax.linalg.triangular_solve(
        factor, inner, left_side=False, lower=True, transpose_a=False
    )


def on_device(train_grads, query_grads, damping):
    layers_here, local_rows, coords = train_grads.shape
    total_rows = local_rows * lax.axis_size("ex")
    half_rows = local_rows // lax.axis_size("pb")
    own_rows = lax.dynamic_slice_in_dim(train_grads, lax.axis_index("pb") * half_rows, half_rows, 1)
    partial_gram = jnp.einsum("lnp,lnq->lpq", own_rows, own_rows, precision=lax.Precision.HIGHEST)
    gram_matrix = lax.psum(partial_gram, ("ex", "pb"))
    identity = jnp.eye(coords, dtype=jnp.float32)
    fisher = gram_matrix / total_rows + damping[:, None, None] * identity[None]
    factor = jnp.linalg.cholesky(fisher)
    queries = query_grads[:, 0]
    solved = solve_rows(factor, queries)
    score_tile = jnp.einsum(
        "lnp,lkp->nk",
        train_grads,
        lax.all_gather(solved, "ex", axis=1, tiled=True),
        precision=lax.Precision.HIGHEST,
    )
    shares = lax.psum_scatter(score_tile, "layer", scatter_dimension=1, tiled=True)
    return shares[:, None, :]


def solution(mesh):
    in_specs = (
        P("layer", ("groups", "ex"), None),
        P("layer", "pb", ("groups", "ex"), None),
        P("layer"),
    )
    out_specs = P(("groups", "ex"), "pb", "layer")
    return jax.shard_map(
        on_device, mesh=mesh, in_specs=in_specs, out_specs=out_specs, check_vma=False
    )
```

profile of v0, /device:TPU:0, one launch (start us, length us, event | category | flops | bytes accessed | tf_op | source)
XLA Modules:
  0.0 545.7 jit_solution(9678609055191033883)
XLA Ops:
  7.5 5.0 convolution_bitcast_fusion
  13.3 113.3 %all-reduce.3.cloned.1.call-done = f32[1,1024,1024]{1,2,0:T(8,128)} async-done(((f32[1,1024,1024]{1,2,0:T(8,128)}), f32[1,1024,1024]{1,2,0:T(8,128)}) %all-reduce.3.cloned.1.call-update) | async-done | bytes 4194320 | tf_op jit(solution)/shard_map/psum | solution.py:22
  126.6 5.1 select_add_fusion
  131.7 5.6 %copy.5 = f32[1,1024,1024]{2,1,0:T(8,128)} copy(f32[1,1024,1024]{1,2,0:T(8,128)} %select_add_fusion) | data formatting | bytes 8388608 | tf_op jit(solution)/shard_map/add | solution.py:24
  137.3 4.5 fusion
  141.8 1.9 copy-done.1
  143.7 11.7 %custom-call.72 = f32[1,128,128]{2,1,0:T(8,128)S(1)} custom-call(f32[1,128,128]{2,1,0:T(8,128)S(1)} %cholesky.582), custom_call_target="Cholesky" | custom-call | tf_op jit(solution)/shard_map/jit(cholesky)/cholesky | solution.py:25
  155.6 9.8 %custom-call.73 = f32[1,1,128,128]{2,3,1,0:T(8,128)S(1)} custom-call(f32[1,1,128,128]{3,2,1,0:T(8,128)S(1)} %get-tuple-element.40), custom_call_target="InvertDiagBlocksLowerTriangular" | custom-call | tf_op jit(solution)/shard_map/jit(cholesky)/cholesky | solution.py:25
  165.4 1.5 fusion.34
  167.1 1.5 fusion.3
  168.7 11.7 %custom-call.74 = f32[1,128,128]{2,1,0:T(8,128)S(1)} custom-call(f32[1,128,128]{2,1,0:T(8,128)S(1)} %cholesky.586), custom_call_target="Cholesky" | custom-call | tf_op jit(solution)/shard_map/jit(cholesky)/cholesky | solution.py:25
  181.1 2.5 cholesky.248
  184.4 9.8 %custom-call.75 = f32[1,1,128,128]{2,3,1,0:T(8,128)S(1)} custom-call(f32[1,1,128,128]{3,2,1,0:T(8,128)S(1)} %get-tuple-element.38), custom_call_target="InvertDiagBlocksLowerTriangular" | custom-call | tf_op jit(solution)/shard_map/jit(cholesky)/cholesky | solution.py:25
  194.8 1.3 fusion.4
  196.1 2.7 fusion.6
  198.9 11.7 %custom-call.76 = f32[1,128,128]{2,1,0:T(8,128)S(1)} custom-call(f32[1,128,128]{2,1,0:T(8,128)S(1)} %cholesky.591), custom_call_target="Cholesky" | custom-call | tf_op jit(solution)/shard_map/jit(cholesky)/cholesky | solution.py:25
  211.3 9.8 %custom-call.77 = f32[1,1,128,128]{2,3,1,0:T(8,128)S(1)} custom-call(f32[1,1,128,128]{3,2,1,0:T(8,128)S(1)} %get-tuple-element.36), custom_call_target="InvertDiagBlocksLowerTriangular" | custom-call | tf_op jit(solution)/shard_map/jit(cholesky)/cholesky | solution.py:25
  221.2 1.3 fusion.5
  222.4 3.3 fusion.8
  225.7 11.7 %custom-call.78 = f32[1,128,128]{2,1,0:T(8,128)S(1)} custom-call(f32[1,128,128]{2,1,0:T(8,128)S(1)} %cholesky.596), custom_call_target="Cholesky" | custom-call | tf_op jit(solution)/shard_map/jit(cholesky)/cholesky | solution.py:25
  238.2 9.8 %custom-call.79 = f32[1,1,128,128]{2,3,1,0:T(8,128)S(1)} custom-call(f32[1,1,128,128]{3,2,1,0:T(8,128)S(1)} %get-tuple-element.34), custom_call_target="InvertDiagBlocksLowerTriangular" | custom-call | tf_op jit(solution)/shard_map/jit(cholesky)/cholesky | solution.py:25
  248.0 1.1 fusion.7
  249.2 3.1 fusion.9
  252.3 11.9 %custom-call.80 = f32[1,128,128]{2,1,0:T(8,128)S(1)} custom-call(f32[1,128,128]{2,1,0:T(8,128)S(1)} %cholesky.601), custom_call_target="Cholesky" | custom-call | tf_op jit(solution)/shard_map/jit(cholesky)/cholesky | solution.py:25
  265.0 9.8 %custom-call.81 = f32[1,1,128,128]{2,3,1,0:T(8,128)S(1)} custom-call(f32[1,1,128,128]{3,2,1,0:T(8,128)S(1)} %get-tuple-element.32), custom_call_target="InvertDiagBlocksLowerTriangular" | custom-call | tf_op jit(solution)/shard_map/jit(cholesky)/cholesky | solution.py:25
  274.8 1.1 fusion.13
  275.9 3.1 fusion.14
  279.0 11.7 %custom-call.82 = f32[1,128,128]{2,1,0:T(8,128)S(1)} custom-call(f32[1,128,128]{2,1,0:T(8,128)S(1)} %cholesky.606), custom_call_target="Cholesky" | custom-call | tf_op jit(solution)/shard_map/jit(cholesky)/cholesky | solution.py:25
  291.5 9.8 %custom-call.83 = f32[1,1,128,128]{2,3,1,0:T(8,128)S(1)} custom-call(f32[1,1,128,128]{3,2,1,0:T(8,128)S(1)} %get-tuple-element.30), custom_call_target="InvertDiagBlocksLowerTriangular" | custom-call | tf_op jit(solution)/shard_map/jit(cholesky)/cholesky | solution.py:25
  301.3 1.0 fusion.15
  302.3 3.1 fusion.16
  305.4 11.7 %custom-call.84 = f32[1,128,128]{2,1,0:T(8,128)S(1)} custom-call(f32[1,128,128]{2,1,0:T(8,128)S(1)} %cholesky.611), custom_call_target="Cholesky" | custom-call | tf_op jit(solution)/shard_map/jit(cholesky)/cholesky | solution.py:25
  317.9 9.8 %custom-call.85 = f32[1,1,128,128]{2,3,1,0:T(8,128)S(1)} custom-call(f32[1,1,128,128]{3,2,1,0:T(8,128)S(1)} %get-tuple-element.28), custom_call_target="InvertDiagBlocksLowerTriangular" | custom-call | tf_op jit(solution)/shard_map/jit(cholesky)/cholesky | solution.py:25
  328.6 2.1 fusion.18
  330.7 11.7 %custom-call.86 = f32[1,128,128]{2,1,0:T(8,128)S(1)} custom-call(f32[1,128,128]{2,1,0:T(8,128)S(1)} %fusion.18), custom_call_target="Cholesky" | custom-call | tf_op jit(solution)/shard_map/jit(cholesky)/cholesky | solution.py:25
  352.9 4.9 select_select_fusion
  357.8 23.7 %while.1 = (s32[]{:T(128)}, f32[1,1024,1024]{1,2,0:T(8,128)}, s32[8,2]{0,1:T(2,128)S(1)}, f32[8,1,128,128]{3,2,1,0:T(8,128)S(1)}, s32[]{:T(128)}) while((s32[]{:T(128)}, f32[1,1024,1024]{1,2,0:T(8,128)}, s32[8,2]{0,1:T(2,128)S(1)}, f32[8,1,128,128]{3,2,1,0:T(8,128)S(1)}, s32[]{:T(128)}) %tuple.49), condition=%wide.while_cond, body=%wide.while_body.sunk | while | flops 2 | bytes 393333 | solution.py:8
  358.4 2.2 constant_dynamic-slice_fusion.5
  361.4 2.2 constant_dynamic-slice_fusion.5
  364.4 2.2 constant_dynamic-slice_fusion.5
  367.3 2.2 constant_dynamic-slice_fusion.5
  370.3 2.2 constant_dynamic-slice_fusion.5
  373.3 2.2 constant_dynamic-slice_fusion.5
  376.3 2.2 constant_dynamic-slice_fusion.5
  379.3 2.2 constant_dynamic-slice_fusion.5
  381.5 78.8 %custom-call.87 = f32[1,8,128,128]{2,3,1,0:T(8,128)S(1)} custom-call(f32[1,8,128,128]{3,2,1,0:T(8,128)S(1)} %bitcast.460), custom_call_target="InvertDiagBlocksLowerTriangular" | custom-call | tf_op jit(solution)/shard_map/triangular_solve | solution.py:8
  460.5 1.0 fusion.27
  461.7 1.1 fusion.25
  463.0 1.2 fusion.23
  464.3 1.2 fusion.21
  465.7 1.3 fusion.33
  467.2 1.3 fusion.31
  468.7 1.4 fusion.29
  470.5 1.1 convolution_subtract_fusion.3
  471.7 1.2 convolution_subtract_fusion.2
  473.1 1.3 convolution_subtract_fusion.1
  474.6 1.3 convolution_subtract_fusion
  476.2 1.4 convolution_subtract_fusion.6
  477.9 1.5 convolution_subtract_fusion.5
  479.7 1.6 convolution_subtract_fusion.4
  482.3 40.7 %all-gather.2.cloned.1.call-done = f32[1,512,1024]{2,1,0:T(8,128)} async-done(((f32[1,32,1024]{2,1,0:T(8,128)}), f32[1,512,1024]{2,1,0:T(8,128)}) %all-gather.2.cloned.1.call-update) | async-done | bytes 2097168 | tf_op jit(solution)/shard_map/all_gather | solution.py:31
  523.0 4.4 fusion.10
  527.5 9.9 %reduce-scatter.2.cloned.1.call-done = f32[96,256]{1,0:T(8,128)} async-done(((f32[96,512]{1,0:T(8,128)}), f32[96,256]{1,0:T(8,128)}) %reduce-scatter.2.cloned.1.call-update) | async-done | bytes 98320 | tf_op jit(solution)/shard_map/reduce_scatter | solution.py:34
  537.4 1.6 copy.22
  (126 shorter events, 23.3 us)
Async XLA Ops:
  6.5 1.0 copy-start
  6.5 120.0 %all-reduce.3.cloned.1.call-start = ((), (), s32[]{:S(2)}) async-start(), calls=%async_computation.1 | async-start | bytes 8388608 | tf_op jit(solution)/shard_map/psum | solution.py:22
  12.6 510.4 %all-gather.2.cloned.1.call-start = ((), (), s32[]{:S(2)}) async-start(), calls=%async_computation.2 | async-start | bytes 2228224 | tf_op jit(solution)/shard_map/all_gather | solution.py:31
  141.8 1.9 copy-start.1
  352.9 107.4 %copy-start.3 = (f32[1,1,32,1024]{3,2,1,0:T(8,128)S(1)}, f32[1,1,32,1024]{3,2,1,0:T(8,128)}, u32[]{:S(2)}) copy-start(f32[1,1,32,1024]{3,2,1,0:T(8,128)} %param.4) | copy-start | bytes 393220
  481.6 0.7 copy-start.2
  482.3 55.1 %reduce-scatter.2.cloned.1.call-start = ((), (), s32[]{:S(2)}) async-start(), calls=%async_computation.3 | async-start | bytes 294912 | tf_op jit(solution)/shard_map/reduce_scatter | solution.py:34
Sparse Core Ops, SparseCore 0:
  12.7 113.8 all-reduce.2
  482.4 40.5 all-gather.1
  527.6 9.7 reduce-scatter.1
where the time goes:
time: 550 us; the launch traced here: 546 us
  other arithmetic  261 us (47%)
  waiting for transfers between devices  164 us (30%)
  matrix products  57.3 us (10%)
  local copies, waits for them, and re-layouts  43.8 us (8%)
  between operations  19.7 us (4%)
    another operation x30, other arithmetic, on_device(): factor = jnp.linalg.cholesky(fisher)  168 us
    psum x1, waiting for transfers between devices, on_device(): gram_matrix = lax.psum(partial_gram, ('ex', 'pb'))  113 us
    another operation x3, other arithmetic, solve_rows(): lax.linalg.triangular_solve(factor, rows_in, left_side=False, lower=True,...  83.6 us
    all_gather x1, waiting for transfers between devices, on_device(): lax.all_gather(solved, 'ex', axis=1, tiled=True)  40.7 us
    another operation x14, matrix products, on_device(): factor = jnp.linalg.cholesky(fisher)  27.2 us
    another operation x40, local copies, waits for them, and re-layouts  23.5 us
  transfers between devices with their start and end apart: 3, of which 3 were waited for; matrix products, arithmetic and copies ran while one was open for 0% of the time, Pallas kernels for 0%

commit v1 on v0

--- a/solution.py
+++ b/solution.py
@@ -2,6 +2,7 @@
 import jax.numpy as jnp
 from jax import lax
 from jax.sharding import PartitionSpec as P
+from jax.lax import axis_index, axis_size, ppermute
 
 
 def solve_rows(factor, rows_in):
@@ -25,12 +26,28 @@
     factor = jnp.linalg.cholesky(fisher)
     queries = query_grads[:, 0]
     solved = solve_rows(factor, queries)
-    score_tile = jnp.einsum(
-        "lnp,lkp->nk",
-        train_grads,
-        lax.all_gather(solved, "ex", axis=1, tiled=True),
-        precision=lax.Precision.HIGHEST,
-    )
+    taken_in = axis_index("ex")
+    near = axis_size("ex")
+    outer, met_up, current_value = (near, taken_in, solved.shape[1])
+    q_next = e_next = solved
+    heard, r_now = ([], [])
+    for jj in range(outer // 2 + 1):
+        placed = jnp.einsum("lnp,lkp->nk", train_grads, q_next, precision=lax.Precision.HIGHEST)
+        heard.append(placed)
+        if 0 < jj < outer - outer // 2:
+            r_now.append(
+                jnp.einsum("lnp,lkp->nk", train_grads, e_next, precision=lax.Precision.HIGHEST)
+            )
+        all_blocks = []
+        for dev in range(outer):
+            all_blocks.append((dev, (dev + 1) % outer))
+        q_next = ppermute(q_next, "ex", all_blocks)
+        pieces_in = []
+        for dev in range(outer):
+            pieces_in.append((dev, (dev - 1) % outer))
+        e_next = ppermute(e_next, "ex", pieces_in)
+    tile_out = jnp.concatenate([*heard[::-1], *r_now], axis=1)
+    score_tile = jnp.roll(tile_out, shift=(met_up - outer // 2) * heard[0].shape[1], axis=1)
     shares = lax.psum_scatter(score_tile, "layer", scatter_dimension=1, tiled=True)
     return shares[:, None, :]
 

time: 550 us -> 570 us (1.036)
  starting transfers between devices: 0.09 us -> 31.4 us
  waiting for transfers between devices: 164 us -> 148 us
    all_gather x1 -> x0, waiting for transfers between devices: 40.7 us -> none  [on_device(): lax.all_gather(solved, 'ex', axis=1, tiled=True)]
    ppermute x0 -> x15, starting transfers between devices: none -> 31.4 us  [the longest x7 31.3 us: on_device(): e_next = ppermute(e_next, 'ex', pieces_in)]
    ppermute x0 -> x15, waiting for transfers between devices: none -> 26 us  [the longest x8 26 us: on_device(): q_next = ppermute(q_next, 'ex', all_blocks)]
  transfers between devices with their start and end apart: 3 -> 17, of which waited for: 3 -> 10; matrix products, arithmetic and copies ran while one was open for 0% -> 1% of each run, Pallas kernels for 0% -> 0%
where the time goes in v1:
time: 570 us; the launch traced here: 566 us
  other arithmetic  261 us (46%)
  waiting for transfers between devices  148 us (26%)
  matrix products  60.8 us (11%)
  local copies, waits for them, and re-layouts  43.9 us (8%)
  starting transfers between devices  31.4 us (6%)
  between operations  20.3 us (4%)
    another operation x30, other arithmetic, on_device(): factor = jnp.linalg.cholesky(fisher)  168 us
    psum x1, waiting for transfers between devices, on_device(): gram_matrix = lax.psum(partial_gram, ('ex', 'pb'))  113 us
    another operation x3, other arithmetic, solve_rows(): lax.linalg.triangular_solve(factor, rows_in, left_side=False, lower=True,...  83.7 us
    ppermute x7, starting transfers between devices, on_device(): e_next = ppermute(e_next, 'ex', pieces_in)  31.3 us
    another operation x14, matrix products, on_device(): factor = jnp.linalg.cholesky(fisher)  26.9 us
    ppermute x8, waiting for transfers between devices, on_device(): q_next = ppermute(q_next, 'ex', all_blocks)  26 us
    another operation x40, local copies, waits for them, and re-layouts  23.5 us
  transfers between devices with their start and end apart: 17, of which 10 were waited for; matrix products, arithmetic and copies ran while one was open for 1% of the time, Pallas kernels for 0%

profile of v1, /device:TPU:0, one launch (start us, length us, event | category | flops | bytes accessed | tf_op | source)
XLA Modules:
  0.0 566.2 jit_solution(15708218522211460485)
XLA Ops:
  7.5 5.0 convolution_bitcast_fusion
  13.3 113.3 %all-reduce.3.cloned.1.call-done = f32[1,1024,1024]{1,2,0:T(8,128)} async-done(((f32[1,1024,1024]{1,2,0:T(8,128)}), f32[1,1024,1024]{1,2,0:T(8,128)}) %all-reduce.3.cloned.1.call-update) | async-done | bytes 4194320 | tf_op jit(solution)/shard_map/psum | solution.py:23
  126.6 5.1 select_add_fusion
  131.7 5.9 %copy.5 = f32[1,1024,1024]{2,1,0:T(8,128)} copy(f32[1,1024,1024]{1,2,0:T(8,128)} %select_add_fusion) | data formatting | bytes 8388608 | tf_op jit(solution)/shard_map/add | solution.py:25
  137.6 4.5 fusion
  142.1 1.9 copy-done.1
  144.0 11.7 %custom-call.72 = f32[1,128,128]{2,1,0:T(8,128)S(1)} custom-call(f32[1,128,128]{2,1,0:T(8,128)S(1)} %cholesky.582), custom_call_target="Cholesky" | custom-call | tf_op jit(solution)/shard_map/jit(cholesky)/cholesky | solution.py:26
  155.9 9.8 %custom-call.73 = f32[1,1,128,128]{2,3,1,0:T(8,128)S(1)} custom-call(f32[1,1,128,128]{3,2,1,0:T(8,128)S(1)} %get-tuple-element.40), custom_call_target="InvertDiagBlocksLowerTriangular" | custom-call | tf_op jit(solution)/shard_map/jit(cholesky)/cholesky | solution.py:26
  165.7 1.5 fusion.29
  167.4 1.5 fusion.1
  169.0 11.7 %custom-call.74 = f32[1,128,128]{2,1,0:T(8,128)S(1)} custom-call(f32[1,128,128]{2,1,0:T(8,128)S(1)} %cholesky.586), custom_call_target="Cholesky" | custom-call | tf_op jit(solution)/shard_map/jit(cholesky)/cholesky | solution.py:26
  181.0 2.5 cholesky.248
  184.3 9.8 %custom-call.75 = f32[1,1,128,128]{2,3,1,0:T(8,128)S(1)} custom-call(f32[1,1,128,128]{3,2,1,0:T(8,128)S(1)} %get-tuple-element.38), custom_call_target="InvertDiagBlocksLowerTriangular" | custom-call | tf_op jit(solution)/shard_map/jit(cholesky)/cholesky | solution.py:26
  196.1 2.7 fusion.4
  198.8 11.7 %custom-call.76 = f32[1,128,128]{2,1,0:T(8,128)S(1)} custom-call(f32[1,128,128]{2,1,0:T(8,128)S(1)} %cholesky.591), custom_call_target="Cholesky" | custom-call | tf_op jit(solution)/shard_map/jit(cholesky)/cholesky | solution.py:26
  211.3 9.8 %custom-call.77 = f32[1,1,128,128]{2,3,1,0:T(8,128)S(1)} custom-call(f32[1,1,128,128]{3,2,1,0:T(8,128)S(1)} %get-tuple-element.36), custom_call_target="InvertDiagBlocksLowerTriangular" | custom-call | tf_op jit(solution)/shard_map/jit(cholesky)/cholesky | solution.py:26
  222.3 3.3 fusion.6
  225.7 11.7 %custom-call.78 = f32[1,128,128]{2,1,0:T(8,128)S(1)} custom-call(f32[1,128,128]{2,1,0:T(8,128)S(1)} %cholesky.596), custom_call_target="Cholesky" | custom-call | tf_op jit(solution)/shard_map/jit(cholesky)/cholesky | solution.py:26
  238.2 9.8 %custom-call.79 = f32[1,1,128,128]{2,3,1,0:T(8,128)S(1)} custom-call(f32[1,1,128,128]{3,2,1,0:T(8,128)S(1)} %get-tuple-element.34), custom_call_target="InvertDiagBlocksLowerTriangular" | custom-call | tf_op jit(solution)/shard_map/jit(cholesky)/cholesky | solution.py:26
  249.1 3.2 fusion.7
  252.3 12.1 %custom-call.80 = f32[1,128,128]{2,1,0:T(8,128)S(1)} custom-call(f32[1,128,128]{2,1,0:T(8,128)S(1)} %cholesky.601), custom_call_target="Cholesky" | custom-call | tf_op jit(solution)/shard_map/jit(cholesky)/cholesky | solution.py:26
  265.1 9.8 %custom-call.81 = f32[1,1,128,128]{2,3,1,0:T(8,128)S(1)} custom-call(f32[1,1,128,128]{3,2,1,0:T(8,128)S(1)} %get-tuple-element.32), custom_call_target="InvertDiagBlocksLowerTriangular" | custom-call | tf_op jit(solution)/shard_map/jit(cholesky)/cholesky | solution.py:26
  276.1 3.1 fusion.9
  279.2 11.7 %custom-call.82 = f32[1,128,128]{2,1,0:T(8,128)S(1)} custom-call(f32[1,128,128]{2,1,0:T(8,128)S(1)} %cholesky.606), custom_call_target="Cholesky" | custom-call | tf_op jit(solution)/shard_map/jit(cholesky)/cholesky | solution.py:26
  291.7 9.8 %custom-call.83 = f32[1,1,128,128]{2,3,1,0:T(8,128)S(1)} custom-call(f32[1,1,128,128]{3,2,1,0:T(8,128)S(1)} %get-tuple-element.30), custom_call_target="InvertDiagBlocksLowerTriangular" | custom-call | tf_op jit(solution)/shard_map/jit(cholesky)/cholesky | solution.py:26
  302.4 2.8 fusion.11
  305.3 11.7 %custom-call.84 = f32[1,128,128]{2,1,0:T(8,128)S(1)} custom-call(f32[1,128,128]{2,1,0:T(8,128)S(1)} %cholesky.611), custom_call_target="Cholesky" | custom-call | tf_op jit(solution)/shard_map/jit(cholesky)/cholesky | solution.py:26
  317.8 9.8 %custom-call.85 = f32[1,1,128,128]{2,3,1,0:T(8,128)S(1)} custom-call(f32[1,1,128,128]{3,2,1,0:T(8,128)S(1)} %get-tuple-element.28), custom_call_target="InvertDiagBlocksLowerTriangular" | custom-call | tf_op jit(solution)/shard_map/jit(cholesky)/cholesky | solution.py:26
  328.5 2.1 fusion.13
  330.6 11.7 %custom-call.86 = f32[1,128,128]{2,1,0:T(8,128)S(1)} custom-call(f32[1,128,128]{2,1,0:T(8,128)S(1)} %fusion.13), custom_call_target="Cholesky" | custom-call | tf_op jit(solution)/shard_map/jit(cholesky)/cholesky | solution.py:26
  352.9 4.9 select_select_fusion
  357.8 23.7 %while.1 = (s32[]{:T(128)}, f32[1,1024,1024]{1,2,0:T(8,128)}, s32[8,2]{0,1:T(2,128)S(1)}, f32[8,1,128,128]{3,2,1,0:T(8,128)S(1)}, s32[]{:T(128)}) while((s32[]{:T(128)}, f32[1,1024,1024]{1,2,0:T(8,128)}, s32[8,2]{0,1:T(2,128)S(1)}, f32[8,1,128,128]{3,2,1,0:T(8,128)S(1)}, s32[]{:T(128)}) %tuple.65), condition=%wide.while_cond, body=%wide.while_body.sunk | while | flops 2 | bytes 393333 | solution.py:9
  358.4 2.2 constant_dynamic-slice_fusion.6
  361.4 2.2 constant_dynamic-slice_fusion.6
  364.4 2.2 constant_dynamic-slice_fusion.6
  367.3 2.2 constant_dynamic-slice_fusion.6
  370.3 2.2 constant_dynamic-slice_fusion.6
  373.3 2.2 constant_dynamic-slice_fusion.6
  376.3 2.2 constant_dynamic-slice_fusion.6
  379.2 2.2 constant_dynamic-slice_fusion.6
  381.5 78.8 %custom-call.87 = f32[1,8,128,128]{2,3,1,0:T(8,128)S(1)} custom-call(f32[1,8,128,128]{3,2,1,0:T(8,128)S(1)} %bitcast.627), custom_call_target="InvertDiagBlocksLowerTriangular" | custom-call | tf_op jit(solution)/shard_map/triangular_solve | solution.py:9
  467.2 1.3 fusion.26
  468.7 1.4 fusion.24
  474.6 1.3 convolution_subtract_fusion
  476.2 1.4 convolution_subtract_fusion.6
  477.9 1.5 convolution_subtract_fusion.5
  479.7 1.6 convolution_subtract_fusion.4
  481.7 7.1 %collective-permute-done = f32[1,32,1024]{2,1,0:T(8,128)S(1)} collective-permute-done((f32[1,32,1024]{2,1,0:T(8,128)S(1)}, f32[1,32,1024]{2,1,0:T(8,128)S(1)}, u32[]{:S(2)}, u32[]{:S(2)}) %collective-permute-start) | collective-permute-done | bytes 131104 | tf_op jit(solution)/shard_map/ppermute | solution.py:44
  488.8 4.4 collective-permute-start.8
  493.2 2.7 collective-permute-done.1
  496.0 4.4 collective-permute-start.9
  500.4 2.7 collective-permute-done.2
  503.2 4.4 collective-permute-start.10
  507.6 2.7 collective-permute-done.3
  510.4 4.4 collective-permute-start.11
  514.8 2.7 collective-permute-done.4
  517.5 4.4 collective-permute-start.12
  522.0 2.7 collective-permute-done.5
  524.7 4.4 collective-permute-start.13
  529.2 2.7 collective-permute-done.6
  531.9 4.7 collective-permute-start.14
  536.6 2.4 collective-permute-done.7
  548.3 9.1 %reduce-scatter.2.cloned.1.call-done = f32[96,256]{0,1:T(8,128)} async-done(((f32[96,512]{0,1:T(8,128)}), f32[96,256]{0,1:T(8,128)}) %reduce-scatter.2.cloned.1.call-update) | async-done | bytes 98320 | tf_op jit(solution)/shard_map/reduce_scatter | solution.py:51
  557.4 1.6 copy.22
  (183 shorter events, 46.4 us)
Async XLA Ops:
  6.5 1.0 copy-start
  6.5 120.1 %all-reduce.3.cloned.1.call-start = ((), (), s32[]{:S(2)}) async-start(), calls=%async_computation.1 | async-start | bytes 8388608 | tf_op jit(solution)/shard_map/psum | solution.py:23
  12.6 544.9 %reduce-scatter.2.cloned.1.call-start = ((), (), s32[]{:S(2)}) async-start(), calls=%async_computation.2 | async-start | bytes 393216 | tf_op jit(solution)/shard_map/reduce_scatter | solution.py:51
  142.1 1.9 copy-start.1
  352.9 107.4 %copy-start.2 = (f32[1,1,32,1024]{3,2,1,0:T(8,128)S(1)}, f32[1,1,32,1024]{3,2,1,0:T(8,128)}, u32[]{:S(2)}) copy-start(f32[1,1,32,1024]{3,2,1,0:T(8,128)} %param.4) | copy-start | bytes 393220
  481.6 7.1 %collective-permute-start = (f32[1,32,1024]{2,1,0:T(8,128)S(1)}, f32[1,32,1024]{2,1,0:T(8,128)S(1)}, u32[]{:S(2)}, u32[]{:S(2)}) collective-permute-start(f32[1,32,1024]{2,1,0:T(8,128)S(1)} %constant_dynamic-update-slice_fusion.36), channel_id=1, source_target_pairs={{0,2},{2,4},{4,6},{6,8},{8,10},{10,12},{12,14},{14,16},{16,18},{18... | collective-permute-start | bytes 393224 | tf_op jit(solution)/shard_map/ppermute | solution.py:44
  488.8 7.2 %collective-permute-start.1 = (f32[1,32,1024]{2,1,0:T(8,128)S(1)}, f32[1,32,1024]{2,1,0:T(8,128)S(1)}, u32[]{:S(2)}, u32[]{:S(2)}) collective-permute-start(f32[1,32,1024]{2,1,0:T(8,128)S(1)} %collective-permute-done), channel_id=1, source_target_pairs={{0,2},{2,4},{4,6},{6,8},{8,10},{10,12},{12,14},{14,16},{16,18},{18... | collective-permute-start | bytes 393224 | tf_op jit(solution)/shard_map/ppermute | solution.py:44
  488.8 7.2 %collective-permute-start.8 = (f32[1,32,1024]{2,1,0:T(8,128)S(1)}, f32[1,32,1024]{2,1,0:T(8,128)S(1)}, u32[]{:S(2)}, u32[]{:S(2)}) collective-permute-start(f32[1,32,1024]{2,1,0:T(8,128)S(1)} %constant_dynamic-update-slice_fusion.36), channel_id=1, source_target_pairs={{0,30},{2,0},{4,2},{6,4},{8,6},{10,8},{12,10},{14,12},{16,14},{18,... | collective-permute-start | bytes 393224 | tf_op jit(solution)/shard_map/ppermute | solution.py:48
  496.0 7.2 %collective-permute-start.2 = (f32[1,32,1024]{2,1,0:T(8,128)S(1)}, f32[1,32,1024]{2,1,0:T(8,128)S(1)}, u32[]{:S(2)}, u32[]{:S(2)}) collective-permute-start(f32[1,32,1024]{2,1,0:T(8,128)S(1)} %collective-permute-done.1), channel_id=1, source_target_pairs={{0,2},{2,4},{4,6},{6,8},{8,10},{10,12},{12,14},{14,16},{16,18},{18... | collective-permute-start | bytes 393224 | tf_op jit(solution)/shard_map/ppermute | solution.py:44
  496.0 7.2 %collective-permute-start.9 = (f32[1,32,1024]{2,1,0:T(8,128)S(1)}, f32[1,32,1024]{2,1,0:T(8,128)S(1)}, u32[]{:S(2)}, u32[]{:S(2)}) collective-permute-start(f32[1,32,1024]{2,1,0:T(8,128)S(1)} %collective-permute-done.8), channel_id=1, source_target_pairs={{0,30},{2,0},{4,2},{6,4},{8,6},{10,8},{12,10},{14,12},{16,14},{18,... | collective-permute-start | bytes 393224 | tf_op jit(solution)/shard_map/ppermute | solution.py:48
  503.2 7.2 %collective-permute-start.3 = (f32[1,32,1024]{2,1,0:T(8,128)S(1)}, f32[1,32,1024]{2,1,0:T(8,128)S(1)}, u32[]{:S(2)}, u32[]{:S(2)}) collective-permute-start(f32[1,32,1024]{2,1,0:T(8,128)S(1)} %collective-permute-done.2), channel_id=1, source_target_pairs={{0,2},{2,4},{4,6},{6,8},{8,10},{10,12},{12,14},{14,16},{16,18},{18... | collective-permute-start | bytes 393224 | tf_op jit(solution)/shard_map/ppermute | solution.py:44
  503.2 7.2 %collective-permute-start.10 = (f32[1,32,1024]{2,1,0:T(8,128)S(1)}, f32[1,32,1024]{2,1,0:T(8,128)S(1)}, u32[]{:S(2)}, u32[]{:S(2)}) collective-permute-start(f32[1,32,1024]{2,1,0:T(8,128)S(1)} %collective-permute-done.9), channel_id=1, source_target_pairs={{0,30},{2,0},{4,2},{6,4},{8,6},{10,8},{12,10},{14,12},{16,14},{18,... | collective-permute-start | bytes 393224 | tf_op jit(solution)/shard_map/ppermute | solution.py:48
  510.4 7.2 %collective-permute-start.4 = (f32[1,32,1024]{2,1,0:T(8,128)S(1)}, f32[1,32,1024]{2,1,0:T(8,128)S(1)}, u32[]{:S(2)}, u32[]{:S(2)}) collective-permute-start(f32[1,32,1024]{2,1,0:T(8,128)S(1)} %collective-permute-done.3), channel_id=1, source_target_pairs={{0,2},{2,4},{4,6},{6,8},{8,10},{10,12},{12,14},{14,16},{16,18},{18... | collective-permute-start | bytes 393224 | tf_op jit(solution)/shard_map/ppermute | solution.py:44
  510.4 7.2 %collective-permute-start.11 = (f32[1,32,1024]{2,1,0:T(8,128)S(1)}, f32[1,32,1024]{2,1,0:T(8,128)S(1)}, u32[]{:S(2)}, u32[]{:S(2)}) collective-permute-start(f32[1,32,1024]{2,1,0:T(8,128)S(1)} %collective-permute-done.10), channel_id=1, source_target_pairs={{0,30},{2,0},{4,2},{6,4},{8,6},{10,8},{12,10},{14,12},{16,14},{18,... | collective-permute-start | bytes 393224 | tf_op jit(solution)/shard_map/ppermute | solution.py:48
  517.5 7.2 %collective-permute-start.5 = (f32[1,32,1024]{2,1,0:T(8,128)S(1)}, f32[1,32,1024]{2,1,0:T(8,128)S(1)}, u32[]{:S(2)}, u32[]{:S(2)}) collective-permute-start(f32[1,32,1024]{2,1,0:T(8,128)S(1)} %collective-permute-done.4), channel_id=1, source_target_pairs={{0,2},{2,4},{4,6},{6,8},{8,10},{10,12},{12,14},{14,16},{16,18},{18... | collective-permute-start | bytes 393224 | tf_op jit(solution)/shard_map/ppermute | solution.py:44
  517.5 7.2 %collective-permute-start.12 = (f32[1,32,1024]{2,1,0:T(8,128)S(1)}, f32[1,32,1024]{2,1,0:T(8,128)S(1)}, u32[]{:S(2)}, u32[]{:S(2)}) collective-permute-start(f32[1,32,1024]{2,1,0:T(8,128)S(1)} %collective-permute-done.11), channel_id=1, source_target_pairs={{0,30},{2,0},{4,2},{6,4},{8,6},{10,8},{12,10},{14,12},{16,14},{18,... | collective-permute-start | bytes 393224 | tf_op jit(solution)/shard_map/ppermute | solution.py:48
  524.7 7.2 %collective-permute-start.6 = (f32[1,32,1024]{2,1,0:T(8,128)S(1)}, f32[1,32,1024]{2,1,0:T(8,128)S(1)}, u32[]{:S(2)}, u32[]{:S(2)}) collective-permute-start(f32[1,32,1024]{2,1,0:T(8,128)S(1)} %collective-permute-done.5), channel_id=1, source_target_pairs={{0,2},{2,4},{4,6},{6,8},{8,10},{10,12},{12,14},{14,16},{16,18},{18... | collective-permute-start | bytes 393224 | tf_op jit(solution)/shard_map/ppermute | solution.py:44
  524.7 7.2 %collective-permute-start.13 = (f32[1,32,1024]{2,1,0:T(8,128)S(1)}, f32[1,32,1024]{2,1,0:T(8,128)S(1)}, u32[]{:S(2)}, u32[]{:S(2)}) collective-permute-start(f32[1,32,1024]{2,1,0:T(8,128)S(1)} %collective-permute-done.12), channel_id=1, source_target_pairs={{0,30},{2,0},{4,2},{6,4},{8,6},{10,8},{12,10},{14,12},{16,14},{18,... | collective-permute-start | bytes 393224 | tf_op jit(solution)/shard_map/ppermute | solution.py:48
  531.9 7.1 %collective-permute-start.7 = (f32[1,32,1024]{2,1,0:T(8,128)S(1)}, f32[1,32,1024]{2,1,0:T(8,128)S(1)}, u32[]{:S(2)}, u32[]{:S(2)}) collective-permute-start(f32[1,32,1024]{2,1,0:T(8,128)S(1)} %collective-permute-done.6), channel_id=1, source_target_pairs={{0,2},{2,4},{4,6},{6,8},{8,10},{10,12},{12,14},{14,16},{16,18},{18... | collective-permute-start | bytes 393224 | tf_op jit(solution)/shard_map/ppermute | solution.py:44
  531.9 14.9 %collective-permute-start.14 = (f32[1,32,1024]{2,1,0:T(8,128)S(1)}, f32[1,32,1024]{2,1,0:T(8,128)S(1)}, u32[]{:S(2)}, u32[]{:S(2)}) collective-permute-start(f32[1,32,1024]{2,1,0:T(8,128)S(1)} %collective-permute-done.13), channel_id=1, source_target_pairs={{0,30},{2,0},{4,2},{6,4},{8,6},{10,8},{12,10},{14,12},{16,14},{18,... | collective-permute-start | bytes 393224 | tf_op jit(solution)/shard_map/ppermute | solution.py:48
Sparse Core Ops, SparseCore 0:
  12.7 113.8 all-reduce.2
  548.4 8.9 reduce-scatter.1
